TPU v7x, 32 devices: a whole 2x2x4 slice. The times are simulated.
32 devices in a mesh: dp: 2 (over y), row: 4 (over x, core), col: 4 (over z).
Axes of the slice: x: 2, y: 2, z: 4, core: 2. Of those that a mesh axis runs over, the one named last changes fastest.
Arguments:
- grad_out: bfloat16 [512, 8192], P(('dp', 'col'), 'row'), may hold values from -6 to 6
- saved_hidden: bfloat16 [512, 26624], P(('dp', 'row'), 'col'), may hold values from -0.26367188 to 0.26367188
- down_weight: bfloat16 [26624, 8192], P('col', 'row'), may hold values from -0.0625 to 0.0625
Outputs:
- input_grad: bfloat16 [512, 26624], P(('dp', 'row'), 'col')
- weight_grad: bfloat16 [26624, 8192], P(('col', 'dp'), 'row')
All inputs are finite; a program needn't handle non-finite values.
Results may differ from a plain program's by a relative error of at most 0.001.
Values may be sent and summed in bfloat16 or wider, within the bound.
No kernel may reach another device: no remote copies, remote signals or barrier semaphores. Data moves between devices by JAX's collectives and lax.ppermute only.
A program may use at most 128 MiB of HBM per device.

v0:
```python
import jax
import jax.numpy as jnp
from jax import lax
from jax.sharding import PartitionSpec as P


def local(grad_out, saved_hidden, down_weight):
    local_rows = saved_hidden.shape[0]
    gathered_all = lax.all_gather(grad_out, ("dp", "col"), axis=0, tiled=True)
    copy_count = lax.axis_size("dp")
    row_count = lax.axis_size("row")
    copy_rows = gathered_all.shape[0] // copy_count
    grad_copy = lax.dynamic_slice_in_dim(
        gathered_all, lax.axis_index("dp") * copy_rows, copy_rows, 0
    )
    hidden_parts = lax.all_to_all(saved_hidden, "dp", split_axis=1, concat_axis=0, tiled=True)
    hidden_stack = lax.all_gather(hidden_parts, "row", axis=0, tiled=True)
    hidden_grid = hidden_stack.reshape(row_count, copy_count, local_rows, hidden_stack.shape[1])
    grad_grid = gathered_all.reshape(copy_count, row_count, local_rows, gathered_all.shape[1])
    weight_grad = jnp.einsum(
        "rdtk,drtn->kn", hidden_grid, grad_grid, preferred_element_type=jnp.float32
    )
    input_grad = lax.psum_scatter(
        lax.dot_general(
            grad_copy, down_weight, (((1,), (1,)), ((), ())), preferred_element_type=jnp.float32
        ),
        "row",
        scatter_dimension=0,
        tiled=True,
    )
    return (input_grad.astype(jnp.bfloat16), weight_grad.astype(jnp.bfloat16))


def solution(mesh):
    placed = (P(("dp", "col"), "row"), P(("dp", "row"), "col"), P("col", "row"))
    return jax.shard_map(
        local,
        mesh=mesh,
        in_specs=placed,
        out_specs=(P(("dp", "row"), "col"), P(("col", "dp"), "row")),
        check_vma=False,
    )
```

profile of v0, /device:TPU:0, one launch (start us, length us, event | category | flops | bytes accessed | tf_op | source)
XLA Modules:
  0.0 167.5 jit_solution(16563208441328073580)
XLA Ops:
  7.2 0.0 all-gather.3.cloned.1.call-start
  7.2 0.7 all-gather.3.cloned.1.call-update
  7.9 0.0 all-gather.5.cloned.1.call-start
  7.9 1.2 copy.15
  9.2 18.8 %all_to_all.19 = bf16[64,2,3328]{2,0,1:T(8,128)(2,1)} all-to-all(bf16[64,2,3328]{2,0,1:T(8,128)(2,1)S(1)} %bitcast.16), channel_id=1, replica_groups=mesh['dp'=2,'row'=4,'col'=4] {'dp'}, dimensions={1} | all-to-all | bytes 1703936 | tf_op jit(solution)/shard_map/all_to_all | solution.py:16
  28.0 0.0 all-gather.5.cloned.1.call-update
  28.0 0.0 reduce-scatter.2.cloned.1.call-start
  28.1 35.4 %all-gather.3.cloned.1.call-done = bf16[512,2048]{1,0:T(8,128)(2,1)} async-done(((bf16[64,2048]{1,0:T(8,128)(2,1)}), bf16[512,2048]{1,0:T(8,128)(2,1)}) %all-gather.3.cloned.1.call-update) | async-done | bytes 2097168 | tf_op jit(solution)/shard_map/all_gather | solution.py:9
  63.5 16.8 %fusion.1 = f32[256,6656]{1,0:T(8,128)} fusion(bf16[6656,2048]{1,0:T(8,128)(2,1)} %param.5, bf16[512,2048]{1,0:T(8,128)(2,1)} %all-gather.3.cloned.1.call-done, s32[]{:T(128)S(6)} %select_n.3), kind=kOutput, calls=%fused_computation.2 | convolution fusion | flops 6979321856 | bytes 35127300 | tf_op jit(solution)/shard_map/dot_general | solution.py:24
  80.2 0.0 copy-start
  80.2 0.0 reduce-scatter.2.cloned.1.call-update
  80.3 13.3 %all-gather.5.cloned.1.call-done = bf16[512,3328]{1,0:T(8,128)(2,1)} async-done(((bf16[128,3328]{1,0:T(8,128)(2,1)}), bf16[512,3328]{1,0:T(8,128)(2,1)}) %all-gather.5.cloned.1.call-update) | async-done | bytes 3407888 | tf_op jit(solution)/shard_map/all_gather | solution.py:17
  93.6 0.0 copy-done
  93.6 13.3 %bitcast_convert_fusion = bf16[3328,2048]{1,0:T(8,128)(2,1)} fusion(bf16[2,4,64,2048]{3,2,1,0:T(8,128)(2,1)S(1)} %bitcast.19, bf16[4,2,64,3328]{3,2,1,0:T(8,128)(2,1)} %bitcast.18), kind=kOutput, calls=%fused_computation | convolution fusion | flops 6986137600 | bytes 19136512 | tf_op jit(solution)/shard_map/rdtk,drtn->kn/dot_general | solution.py:20
  106.9 51.6 %reduce-scatter.2.cloned.1.call-done = f32[64,6656]{1,0:T(8,128)} async-done(((f32[256,6656]{1,0:T(8,128)}), f32[64,6656]{1,0:T(8,128)}) %reduce-scatter.2.cloned.1.call-update) | async-done | bytes 1703952 | tf_op jit(solution)/shard_map/reduce_scatter | solution.py:23
  158.6 2.4 %convert_element_type.6 = bf16[64,6656]{1,0:T(8,128)(2,1)} convert(f32[64,6656]{1,0:T(8,128)} %reduce-scatter.2.cloned.1.call-done) | non-fusion elementwise | flops 425984 | bytes 2555904 | tf_op jit(solution)/shard_map/convert_element_type | solution.py:31
Async XLA Ops:
  7.2 56.3 %all-gather.3.cloned.1.call-start = ((), (), s32[]{:S(2)}) async-start(), calls=%async_computation.2 | async-start | bytes 2359296 | tf_op jit(solution)/shard_map/all_gather | solution.py:9
  7.9 85.7 %all-gather.5.cloned.1.call-start = ((), (), s32[]{:S(2)}) async-start(), calls=%async_computation.4 | async-start | bytes 4259840 | tf_op jit(solution)/shard_map/all_gather | solution.py:17
  28.0 130.6 %reduce-scatter.2.cloned.1.call-start = ((), (), s32[]{:S(2)}) async-start(), calls=%async_computation.3 | async-start | bytes 8519680 | tf_op jit(solution)/shard_map/reduce_scatter | solution.py:23
  80.2 13.4 %copy-start = (bf16[512,2048]{1,0:T(8,128)(2,1)S(1)}, bf16[512,2048]{1,0:T(8,128)(2,1)}, u32[]{:S(2)}) copy-start(bf16[512,2048]{1,0:T(8,128)(2,1)} %all-gather.3.cloned.1.call-done) | copy-start | bytes 6291460
Sparse Core Ops, SparseCore 0:
  10.1 53.3 all-gather.2
  65.0 28.5 all-gather.4
  96.1 62.3 reduce-scatter.1
where the time goes:
time: 168 us
  waiting for transfers between devices  101 us (60%)
  matrix products  30.1 us (18%)
  blocking collectives  18.8 us (11%)
  between operations  13.8 us (8%)
  other arithmetic  2.44 us (1%)
    reduce_scatter x1, waiting for transfers between devices, local(): lax.psum_scatter(lax.dot_general(grad_copy, down_weight, (((1,), (1,)), (...  51.6 us
    all_gather x1, waiting for transfers between devices, local(): gathered_all = lax.all_gather(grad_out, ('dp', 'col'), axis=0, tiled=True)  35.4 us
    all_to_all x1, blocking collectives, local(): lax.all_to_all(saved_hidden, 'dp', split_axis=1, concat_axis=0, tiled=True)  18.8 us
    dot_general x1, matrix products, local(): lax.dot_general(grad_copy, down_weight, (((1,), (1,)), ((), ())), preferr...  16.8 us
    all_gather x1, waiting for transfers between devices, local(): hidden_stack = lax.all_gather(hidden_parts, 'row', axis=0, tiled=True)  13.3 us
    dot_general x1, matrix products, local(): jnp.einsum('rdtk,drtn->kn', hidden_grid, grad_grid, preferred_element_typ...  13.3 us
  transfers between devices with their start and end apart: 3, of which 3 were waited for; matrix products, arithmetic and copies ran while one was open for 19% of the time, Pallas kernels for 0%

commit v1 on v0

--- a/solution.py
+++ b/solution.py
@@ -14,7 +14,12 @@
         gathered_all, lax.axis_index("dp") * copy_rows, copy_rows, 0
     )
     hidden_parts = lax.all_to_all(saved_hidden, "dp", split_axis=1, concat_axis=0, tiled=True)
-    hidden_stack = lax.all_gather(hidden_parts, "row", axis=0, tiled=True)
+    ring = [hidden_parts]
+    for hop in range(3):
+        ring.append(lax.ppermute(ring[-1], "row", [(dev, (dev + 1) % 4) for dev in range(4)]))
+    hidden_stack = jnp.roll(
+        jnp.concatenate(ring[::-1], axis=0), (lax.axis_index("row") + 1) * ring[0].shape[0], axis=0
+    )
     hidden_grid = hidden_stack.reshape(row_count, copy_count, local_rows, hidden_stack.shape[1])
     grad_grid = gathered_all.reshape(copy_count, row_count, local_rows, gathered_all.shape[1])
     weight_grad = jnp.einsum(

time: 168 us -> 180 us (1.071)
  waiting for transfers between devices: 101 us -> 119 us
  blocking collectives: 18.8 us -> 12.3 us
  matrix products: 30.1 us -> 26.1 us
  starting transfers between devices: 0.12 us -> 3.02 us
    ppermute x0 -> x3, waiting for transfers between devices: none -> 63.9 us  [local(): lax.ppermute(ring[-1], 'row', [(dev, (dev + 1) % 4) for dev in range(4)])]
    reduce_scatter x1, waiting for transfers between devices: 51.6 us -> 0.01 us  [local(): lax.psum_scatter(lax.dot_general(grad_copy, down_weight, (((1,), (1,)), (...]
    all_gather x1, waiting for transfers between devices: 35.4 us -> 54 us  [local(): gathered_all = lax.all_gather(grad_out, ('dp', 'col'), axis=0, tiled=True)]
    all_gather x1 -> x0, waiting for transfers between devices: 13.3 us -> none  [local(): hidden_stack = lax.all_gather(hidden_parts, 'row', axis=0, tiled=True)]
    all_to_all x1, blocking collectives: 18.8 us -> 12.3 us  [local(): lax.all_to_all(saved_hidden, 'dp', split_axis=1, concat_axis=0, tiled=True)]
    ppermute x0 -> x3, starting transfers between devices: none -> 2.95 us  [local(): lax.ppermute(ring[-1], 'row', [(dev, (dev + 1) % 4) for dev in range(4)])]
    dot_general x1, matrix products: 13.3 us -> 10.4 us  [local(): jnp.einsum('rdtk,drtn->kn', hidden_grid, grad_grid, preferred_element_typ...]
    unnamed x2 -> x11, local copies, waits for them, and re-layouts: 0.01 us -> 2.62 us
  transfers between devices with their start and end apart: 3 -> 5, of which waited for: 3 -> 4; matrix products, arithmetic and copies ran while one was open for 19% -> 6% of each run, Pallas kernels for 0% -> 0%
where the time goes in v1:
time: 180 us
  waiting for transfers between devices  119 us (66%)
  matrix products  26.1 us (14%)
  between operations  14.1 us (8%)
  blocking collectives  12.3 us (7%)
  starting transfers between devices  3.02 us (2%)
  local copies, waits for them, and re-layouts  2.96 us (2%)
  other arithmetic  2.44 us (1%)
    ppermute x3, waiting for transfers between devices, local(): lax.ppermute(ring[-1], 'row', [(dev, (dev + 1) % 4) for dev in range(4)])  63.9 us
    all_gather x1, waiting for transfers between devices, local(): gathered_all = lax.all_gather(grad_out, ('dp', 'col'), axis=0, tiled=True)  54 us
    dot_general x1, matrix products, local(): lax.dot_general(grad_copy, down_weight, (((1,), (1,)), ((), ())), preferr...  15.6 us
    all_to_all x1, blocking collectives, local(): lax.all_to_all(saved_hidden, 'dp', split_axis=1, concat_axis=0, tiled=True)  12.3 us
    dot_general x1, matrix products, local(): jnp.einsum('rdtk,drtn->kn', hidden_grid, grad_grid, preferred_element_typ...  10.4 us
  transfers between devices with their start and end apart: 5, of which 4 were waited for; matrix products, arithmetic and copies ran while one was open for 6% of the time, Pallas kernels for 0%

profile of v1, /device:TPU:0, one launch (start us, length us, event | category | flops | bytes accessed | tf_op | source)
XLA Modules:
  0.0 179.5 jit_solution(12486035017376318654)
XLA Ops:
  7.2 0.0 all-gather.2.cloned.1.call-start
  7.2 0.7 all-gather.2.cloned.1.call-update
  7.9 0.0 reduce-scatter.2.cloned.1.call-start
  7.9 54.0 %all-gather.2.cloned.1.call-done = bf16[512,2048]{1,0:T(8,128)(2,1)} async-done(((bf16[64,2048]{1,0:T(8,128)(2,1)}), bf16[512,2048]{1,0:T(8,128)(2,1)}) %all-gather.2.cloned.1.call-update) | async-done | bytes 2097168 | tf_op jit(solution)/shard_map/all_gather | solution.py:9
  61.9 15.6 %fusion.1 = f32[256,6656]{1,0:T(8,128)} fusion(bf16[6656,2048]{1,0:T(8,128)(2,1)} %param.5, bf16[512,2048]{1,0:T(8,128)(2,1)} %all-gather.2.cloned.1.call-done, s32[]{:T(128)S(6)} %select_n.16), kind=kOutput, calls=%fused_computation.2 | convolution fusion | flops 6979321856 | bytes 35127300 | tf_op jit(solution)/shard_map/dot_general | solution.py:29
  77.6 0.0 copy-start
  77.6 0.0 reduce-scatter.2.cloned.1.call-update
  77.6 1.1 copy-done
  78.7 0.1 copy.15
  78.8 12.3 %all_to_all.19 = bf16[64,2,3328]{2,0,1:T(8,128)(2,1)S(1)} all-to-all(bf16[64,2,3328]{2,0,1:T(8,128)(2,1)S(1)} %bitcast.19), channel_id=1, replica_groups=mesh['dp'=2,'row'=4,'col'=4] {'dp'}, dimensions={1} | all-to-all | bytes 1703936 | tf_op jit(solution)/shard_map/all_to_all | solution.py:16
  91.1 0.0 collective-permute-start
  91.1 17.8 %collective-permute-done = bf16[128,3328]{1,0:T(8,128)(2,1)S(1)} collective-permute-done((bf16[128,3328]{1,0:T(8,128)(2,1)S(1)}, bf16[128,3328]{1,0:T(8,128)(2,1)S(1)}, u32[]{:S(2)}, u32[]{:S(2)}) %collective-permute-start) | collective-permute-done | bytes 852000 | tf_op jit(solution)/shard_map/ppermute | solution.py:19
  108.9 1.5 collective-permute-start.1
  110.3 29.0 %collective-permute-done.1 = bf16[128,3328]{1,0:T(8,128)(2,1)S(1)} collective-permute-done((bf16[128,3328]{1,0:T(8,128)(2,1)S(1)}, bf16[128,3328]{1,0:T(8,128)(2,1)S(1)}, u32[]{:S(2)}, u32[]{:S(2)}) %collective-permute-start.1) | collective-permute-done | bytes 852000 | tf_op jit(solution)/shard_map/ppermute | solution.py:19
  139.4 1.5 collective-permute-start.2
  140.8 17.1 %collective-permute-done.2 = bf16[128,3328]{1,0:T(8,128)(2,1)S(1)} collective-permute-done((bf16[128,3328]{1,0:T(8,128)(2,1)S(1)}, bf16[128,3328]{1,0:T(8,128)(2,1)S(1)}, u32[]{:S(2)}, u32[]{:S(2)}) %collective-permute-start.2) | collective-permute-done | bytes 852000 | tf_op jit(solution)/shard_map/ppermute | solution.py:19
  158.0 0.1 constant_dynamic-update-slice_fusion.7
  158.0 0.1 constant_dynamic-update-slice_fusion.6
  158.1 0.1 constant_dynamic-update-slice_fusion.5
  158.1 0.1 constant_dynamic-update-slice_fusion.4
  158.2 0.0 copy-start.1
  158.2 0.1 constant_dynamic-update-slice_fusion.3
  158.3 0.1 constant_dynamic-update-slice_fusion.2
  158.4 0.1 constant_dynamic-update-slice_fusion.1
  158.4 0.1 constant_dynamic-update-slice_fusion
  158.5 0.2 constant_dynamic-slice_fusion
  158.7 1.1 copy-done.1
  159.8 10.4 %bitcast_convert_fusion = bf16[3328,2048]{1,0:T(8,128)(2,1)} fusion(bf16[2,4,64,2048]{3,2,1,0:T(8,128)(2,1)S(1)} %bitcast.21, bf16[4,2,64,3328]{3,2,1,0:T(8,128)(2,1)S(1)} %bitcast.18), kind=kOutput, calls=%fused_computation | convolution fusion | flops 6986137600 | bytes 19136512 | tf_op jit(solution)/shard_map/rdtk,drtn->kn/dot_general | solution.py:25
  170.3 0.0 reduce-scatter.2.cloned.1.call-done
  170.3 2.4 %convert_element_type.6 = bf16[64,6656]{1,0:T(8,128)(2,1)} convert(f32[64,6656]{1,0:T(8,128)} %reduce-scatter.2.cloned.1.call-done) | non-fusion elementwise | flops 425984 | bytes 2555904 | tf_op jit(solution)/shard_map/convert_element_type | solution.py:36
Async XLA Ops:
  7.2 54.8 %all-gather.2.cloned.1.call-start = ((), (), s32[]{:S(2)}) async-start(), calls=%async_computation.2 | async-start | bytes 2359296 | tf_op jit(solution)/shard_map/all_gather | solution.py:9
  7.9 162.4 %reduce-scatter.2.cloned.1.call-start = ((), (), s32[]{:S(2)}) async-start(), calls=%async_computation.3 | async-start | bytes 8519680 | tf_op jit(solution)/shard_map/reduce_scatter | solution.py:28
  77.6 1.2 copy-start
  91.1 17.8 %collective-permute-start = (bf16[128,3328]{1,0:T(8,128)(2,1)S(1)}, bf16[128,3328]{1,0:T(8,128)(2,1)S(1)}, u32[]{:S(2)}, u32[]{:S(2)}) collective-permute-start(bf16[128,3328]{1,0:T(8,128)(2,1)S(1)} %bitcast.15), channel_id=1, source_target_pairs={{0,4},{4,8},{8,12},{12,0},{1,5},{5,9},{9,13},{13,1},{2,6},{6,10},{... | collective-permute-start | bytes 2555912 | tf_op jit(solution)/shard_map/ppermute | solution.py:19
  108.9 30.5 %collective-permute-start.1 = (bf16[128,3328]{1,0:T(8,128)(2,1)S(1)}, bf16[128,3328]{1,0:T(8,128)(2,1)S(1)}, u32[]{:S(2)}, u32[]{:S(2)}) collective-permute-start(bf16[128,3328]{1,0:T(8,128)(2,1)S(1)} %collective-permute-done), channel_id=1, source_target_pairs={{0,4},{4,8},{8,12},{12,0},{1,5},{5,9},{9,13},{13,1},{2,6},{6,10},{... | collective-permute-start | bytes 2555912 | tf_op jit(solution)/shard_map/ppermute | solution.py:19
  139.4 18.6 %collective-permute-start.2 = (bf16[128,3328]{1,0:T(8,128)(2,1)S(1)}, bf16[128,3328]{1,0:T(8,128)(2,1)S(1)}, u32[]{:S(2)}, u32[]{:S(2)}) collective-permute-start(bf16[128,3328]{1,0:T(8,128)(2,1)S(1)} %collective-permute-done.1), channel_id=1, source_target_pairs={{0,4},{4,8},{8,12},{12,0},{1,5},{5,9},{9,13},{13,1},{2,6},{6,10},{... | collective-permute-start | bytes 2555912 | tf_op jit(solution)/shard_map/ppermute | solution.py:19
  158.2 1.6 copy-start.1
Sparse Core Ops, SparseCore 0:
  10.1 51.8 all-gather.1
  77.7 76.1 reduce-scatter.1
